TPU v7x, 32 devices: a whole 2x2x4 slice. The times are simulated.
32 devices in a mesh: fsdp: 2 (over core), ctx: 4 (over y, x), tp: 4 (over z).
Axes of the slice: x: 2, y: 2, z: 4, core: 2. Of those that a mesh axis runs over, the one named last changes fastest.
Arguments:
- tokens: bfloat16 [4096, 2048], P(('fsdp', 'ctx')), may hold values from -6 to 6
- attn_gain: bfloat16 [2048], P(('fsdp', 'ctx')), may hold values from 0.099609375 to 1.8984375
- w_query: bfloat16 [2048, 2048], P(('fsdp', 'ctx'), 'tp'), may hold values from -0.125 to 0.125
- w_key: bfloat16 [2048, 256], P(('fsdp', 'ctx'), 'tp'), may hold values from -0.125 to 0.125
- w_value: bfloat16 [2048, 256], P(('fsdp', 'ctx'), 'tp'), may hold values from -0.125 to 0.125
- w_out: bfloat16 [2048, 2048], P('tp', ('fsdp', 'ctx')), may hold values from -1 to 1
- mlp_gain: bfloat16 [2048], P(('fsdp', 'ctx')), may hold values from 0.099609375 to 1.8984375
- w_gate: bfloat16 [2048, 5632], P(('fsdp', 'ctx'), 'tp'), may hold values from -0.125 to 0.125
- w_up: bfloat16 [2048, 5632], P(('fsdp', 'ctx'), 'tp'), may hold values from -0.125 to 0.125
- w_down: bfloat16 [5632, 2048], P('tp', ('fsdp', 'ctx')), may hold values from -0.15625 to 0.15625
- cotangent: bfloat16 [4096, 2048], P(('fsdp', 'ctx')), may hold values from -6 to 6
- positions: int32 [4096], P(('fsdp', 'ctx')), may hold values from 0 to 1023, as said below
- segments: int32 [4096], P(('fsdp', 'ctx')), may hold values from 0 to 4095, as said below
Outputs:
- output: bfloat16 [4096, 2048], P(('fsdp', 'ctx'))
- input_grad: bfloat16 [4096, 2048], P(('fsdp', 'ctx'))
- attn_gain_grad: float32 [2048], P(('fsdp', 'ctx'))
- w_query_grad: float32 [2048, 2048], P(('fsdp', 'ctx'), 'tp')
- w_key_grad: float32 [2048, 256], P(('fsdp', 'ctx'), 'tp')
- w_value_grad: float32 [2048, 256], P(('fsdp', 'ctx'), 'tp')
- w_out_grad: float32 [2048, 2048], P('tp', ('fsdp', 'ctx'))
- mlp_gain_grad: float32 [2048], P(('fsdp', 'ctx'))
- w_gate_grad: float32 [2048, 5632], P(('fsdp', 'ctx'), 'tp')
- w_up_grad: float32 [2048, 5632], P(('fsdp', 'ctx'), 'tp')
- w_down_grad: float32 [5632, 2048], P('tp', ('fsdp', 'ctx'))
Inputs may be any that keep to these rules, and one draw needn't show every extreme that they name: Every sequence is cut into 8 stretches of 128 consecutive positions, laid in increasing order inside a stretch; its stretches lie on one index of fsdp, two on each index of ctx, in an order drawn from the seed; each device holds 4 stretches, those of one sequence side by side. `segments`: A document is a run of consecutive positions of one sequence with one number, 200 to 2000 long except the last of a sequence, which may be shorter; documents of different sequences have different numbers.
All inputs are finite; a program needn't handle non-finite values.
Results may differ from a plain program's by a relative error of at most 0.025.
Values may be sent and summed in bfloat16 or wider, within the bound.
A program may use at most 192 MiB of HBM per device.

v0:
```python
import jax
import jax.numpy as jnp
import numpy as np
from jax import lax
from jax.experimental import pallas as pl
from jax.experimental.pallas import tpu as pltpu
from jax.sharding import PartitionSpec as P

H = 32
KVH = 4
HD = 64


EPSILON = 1e-05
THETA_BASE = 10000.0
MASKED_SCORE = -1e30


def shifted(value, axis, steps):
    count = lax.axis_size(axis)
    pairs = [(source, (source + steps) % count) for source in range(count)]
    return lax.ppermute(value, axis, pairs)


def rope_tables(token_pos, half_size):
    frequency = THETA_BASE ** (-jnp.arange(half_size, dtype=jnp.float32) / half_size)
    angles = token_pos.astype(jnp.float32)[:, None] * frequency[None, :]
    return (jnp.cos(angles), jnp.sin(angles))


def rotate(head_rows, cosine, sine):
    half_size = head_rows.shape[-1] // 2
    first_half = head_rows[..., :half_size]
    second_half = head_rows[..., half_size:]
    cos_rows = cosine[:, None, :]
    sin_rows = sine[:, None, :]
    return jnp.concatenate(
        [
            first_half * cos_rows - second_half * sin_rows,
            second_half * cos_rows + first_half * sin_rows,
        ],
        axis=-1,
    )


def rotate_back(head_rows, cosine, sine):
    half_size = head_rows.shape[-1] // 2
    first_half = head_rows[..., :half_size]
    second_half = head_rows[..., half_size:]
    cos_rows = cosine[:, None, :]
    sin_rows = sine[:, None, :]
    return jnp.concatenate(
        [
            first_half * cos_rows + second_half * sin_rows,
            second_half * cos_rows - first_half * sin_rows,
        ],
        axis=-1,
    )


def project(left_side, right_side):
    return jnp.dot(left_side, right_side, preferred_element_type=jnp.float32)


def project_back(left_side, right_side):
    return lax.dot_general(
        left_side, right_side, (((1,), (1,)), ((), ())), preferred_element_type=jnp.float32
    )


def weight_grad(left_side, right_side):
    return lax.dot_general(
        left_side, right_side, (((0,), (0,)), ((), ())), preferred_element_type=jnp.float32
    )


def rms_norm(rows_in, gain_vec):
    inv_rms = lax.rsqrt(jnp.mean(rows_in * rows_in, axis=-1, keepdims=True) + EPSILON)
    unit_rows = rows_in * inv_rms
    return (unit_rows * gain_vec, unit_rows, inv_rms)


def rms_norm_back(gradient, gain_vec, unit_rows, inv_rms):
    gain_grad = jnp.sum(gradient * unit_rows, axis=0)
    scaled_grad = gradient * gain_vec
    return (
        inv_rms
        * (scaled_grad - unit_rows * jnp.mean(scaled_grad * unit_rows, axis=-1, keepdims=True)),
        gain_grad,
    )


def pair_mask(query_pos, query_seg, key_pos, key_seg):
    return (query_seg[:, None] == key_seg[None, :]) & (key_pos[None, :] <= query_pos[:, None])


def split_block(kv_block, kv_heads):
    key_rows = kv_block[:, : kv_heads * HD].reshape(-1, kv_heads, HD)
    value_rows = kv_block[:, kv_heads * HD :].reshape(-1, kv_heads, HD)
    return (key_rows, value_rows)


def attend_block(state_in, queries, kv_block, visible):
    row_top, row_total, output_sum = state_in
    key_rows, value_rows = split_block(kv_block, queries.shape[1])
    scores = jnp.einsum(
        "qkgd,pkd->kgqp", queries, key_rows, preferred_element_type=jnp.float32
    ) * HD ** (-0.5)
    scores = jnp.where(visible, scores, MASKED_SCORE)
    new_top = jnp.maximum(row_top, jnp.max(scores, axis=-1))
    weights = jnp.where(visible, jnp.exp(scores - new_top[..., None]), 0.0)
    decay_factor = jnp.exp(row_top - new_top)
    row_total = row_total * decay_factor + jnp.sum(weights, axis=-1)
    mixed_heads = jnp.einsum(
        "kgqp,pkd->qkgd",
        weights.astype(jnp.bfloat16),
        value_rows,
        preferred_element_type=jnp.float32,
    )
    output_sum = output_sum * jnp.transpose(decay_factor, (2, 0, 1))[..., None] + mixed_heads
    return (new_top, row_total, output_sum)


def block_grads(queries, out_grad, kv_block, visible, log_total, delta_rows):
    key_rows, value_rows = split_block(kv_block, queries.shape[1])
    scale_factor = HD ** (-0.5)
    scores = (
        jnp.einsum("qkgd,pkd->kgqp", queries, key_rows, preferred_element_type=jnp.float32)
        * scale_factor
    )
    probs_full = jnp.where(
        visible, jnp.exp(jnp.where(visible, scores, MASKED_SCORE) - log_total[..., None]), 0.0
    )
    value_grad = jnp.einsum(
        "kgqp,qkgd->pkd",
        probs_full.astype(jnp.bfloat16),
        out_grad,
        preferred_element_type=jnp.float32,
    )
    prob_grad = jnp.einsum(
        "qkgd,pkd->kgqp", out_grad, value_rows, preferred_element_type=jnp.float32
    )
    score_grad = (probs_full * (prob_grad - delta_rows[..., None])).astype(jnp.bfloat16)
    query_grad = (
        jnp.einsum("kgqp,pkd->qkgd", score_grad, key_rows, preferred_element_type=jnp.float32)
        * scale_factor
    )
    key_grad = (
        jnp.einsum("kgqp,qkgd->pkd", score_grad, queries, preferred_element_type=jnp.float32)
        * scale_factor
    )
    block_rows = kv_block.shape[0]
    return (
        query_grad,
        jnp.concatenate(
            [key_grad.reshape(block_rows, -1), value_grad.reshape(block_rows, -1)], axis=-1
        ),
    )


def shards(
    tokens,
    attn_gain,
    w_query,
    w_key,
    w_value,
    w_out,
    mlp_gain,
    w_gate,
    w_up,
    w_down,
    cotangent,
    positions,
    segments,
):
    token_rows = tokens.shape[0]
    gain_one, query_w, key_w, value_w, out_w = (
        lax.all_gather(attn_gain, ("fsdp", "ctx"), axis=0, tiled=True),
        lax.all_gather(w_query, ("fsdp", "ctx"), axis=0, tiled=True),
        lax.all_gather(w_key, ("fsdp", "ctx"), axis=0, tiled=True),
        lax.all_gather(w_value, ("fsdp", "ctx"), axis=0, tiled=True),
        lax.all_gather(w_out, ("fsdp", "ctx"), axis=1, tiled=True),
    )
    gain_two, gate_w, up_w, down_w = (
        lax.all_gather(mlp_gain, ("fsdp", "ctx"), axis=0, tiled=True),
        lax.all_gather(w_gate, ("fsdp", "ctx"), axis=0, tiled=True),
        lax.all_gather(w_up, ("fsdp", "ctx"), axis=0, tiled=True),
        lax.all_gather(w_down, ("fsdp", "ctx"), axis=1, tiled=True),
    )
    head_count = query_w.shape[1] // HD
    kv_heads = key_w.shape[1] // HD
    groups = H // KVH
    cosine, sine = rope_tables(positions, HD // 2)
    token_float = tokens.astype(jnp.float32)
    gain_one_float = gain_one.astype(jnp.float32)
    normed_one, unit_one, inv_one = rms_norm(token_float, gain_one_float)
    normed_low = normed_one.astype(jnp.bfloat16)
    query_lin = project(normed_low, query_w)
    key_lin = project(normed_low, key_w)
    value_low = project(normed_low, value_w).astype(jnp.bfloat16)
    query_rot = rotate(query_lin.reshape(token_rows, head_count, HD), cosine, sine).astype(
        jnp.bfloat16
    )
    key_rot = rotate(key_lin.reshape(token_rows, kv_heads, HD), cosine, sine).astype(jnp.bfloat16)
    queries = query_rot.reshape(token_rows, kv_heads, groups, HD)
    kv_local = jnp.concatenate([key_rot.reshape(token_rows, kv_heads * HD), value_low], axis=-1)
    key_positions, key_segments = (
        lax.all_gather(positions, "ctx", axis=0, tiled=True),
        lax.all_gather(segments, "ctx", axis=0, tiled=True),
    )
    my_index = lax.axis_index("ctx")
    cycle_size = lax.axis_size("ctx")

    def block_marks(source):
        start_row = source * token_rows
        return pair_mask(
            positions,
            segments,
            lax.dynamic_slice_in_dim(key_positions, start_row, token_rows),
            lax.dynamic_slice_in_dim(key_segments, start_row, token_rows),
        )

    start_state = (
        jnp.full((kv_heads, groups, token_rows), MASKED_SCORE, jnp.float32),
        jnp.zeros((kv_heads, groups, token_rows), jnp.float32),
        jnp.zeros((token_rows, kv_heads, groups, HD), jnp.float32),
    )

    def forward_block(state_in, kv_block, source):
        visible = block_marks(source)
        return attend_block(state_in, queries, kv_block, visible)

    def cycle_step(state_in, step_index):
        attn_state, kv_block = state_in
        attn_state = forward_block(attn_state, kv_block, (my_index - step_index) % cycle_size)
        passed = shifted(kv_block, "ctx", 1)
        return ((attn_state, passed), kv_block)

    (attn_state, last_block), kept_blocks = lax.scan(
        cycle_step, (start_state, kv_local), jnp.arange(cycle_size - 1)
    )
    attn_state = forward_block(attn_state, last_block, (my_index + 1) % cycle_size)
    kv_blocks = jnp.concatenate([kept_blocks, last_block[None]], axis=0)
    sources = (my_index - jnp.arange(cycle_size)) % cycle_size
    row_top, row_total, output_sum = attn_state
    attended = output_sum / jnp.transpose(row_total, (2, 0, 1))[..., None]
    log_total = row_top + jnp.log(row_total)
    attended_low = attended.reshape(token_rows, head_count * HD).astype(jnp.bfloat16)
    middle = token_float + lax.psum(project(attended_low, out_w).astype(jnp.bfloat16), "tp").astype(
        jnp.float32
    )
    gain_two_float = gain_two.astype(jnp.float32)
    normed_two, unit_two, inv_two = rms_norm(middle, gain_two_float)
    normed_two_low = normed_two.astype(jnp.bfloat16)
    gate_lin = project(normed_two_low, gate_w)
    up_lin = project(normed_two_low, up_w)
    hidden_low = (jax.nn.silu(gate_lin) * up_lin).astype(jnp.bfloat16)
    result = middle + lax.psum(project(hidden_low, down_w).astype(jnp.bfloat16), "tp").astype(
        jnp.float32
    )
    output = result.astype(jnp.bfloat16)
    hidden_grad = project_back(cotangent, down_w)
    down_w_grad = weight_grad(hidden_low, cotangent)
    sigmoid_gate = jax.nn.sigmoid(gate_lin)
    gate_grad_low = (
        hidden_grad * up_lin * sigmoid_gate * (1.0 + gate_lin * (1.0 - sigmoid_gate))
    ).astype(jnp.bfloat16)
    up_grad_low = (hidden_grad * gate_lin * sigmoid_gate).astype(jnp.bfloat16)
    normed_two_grad = lax.psum(
        (project_back(gate_grad_low, gate_w) + project_back(up_grad_low, up_w)).astype(
            jnp.bfloat16
        ),
        "tp",
    ).astype(jnp.float32)
    gate_w_grad = weight_grad(normed_two_low, gate_grad_low)
    up_w_grad = weight_grad(normed_two_low, up_grad_low)
    norm_back_two, gain_two_grad = rms_norm_back(normed_two_grad, gain_two_float, unit_two, inv_two)
    middle_grad = cotangent.astype(jnp.float32) + norm_back_two
    middle_low = middle_grad.astype(jnp.bfloat16)
    attended_grad_low = project_back(middle_low, out_w).astype(jnp.bfloat16)
    out_w_grad = weight_grad(attended_low, middle_low)
    out_grad = attended_grad_low.reshape(token_rows, kv_heads, groups, HD)
    delta_rows = jnp.transpose(jnp.sum(out_grad.astype(jnp.float32) * attended, axis=-1), (1, 2, 0))

    def backward_block(kv_block, source):
        visible = block_marks(source)
        return block_grads(queries, out_grad, kv_block, visible, log_total, delta_rows)

    query_start = jnp.zeros((token_rows, kv_heads, groups, HD), jnp.float32)

    def back_step(state_in, pieces):
        query_acc, kv_acc = state_in
        query_term, kv_term = backward_block(pieces[0], pieces[1])
        passed = shifted((kv_acc + kv_term).astype(jnp.bfloat16), "ctx", 1).astype(jnp.float32)
        return ((query_acc + query_term, passed), None)

    (query_grad, kv_grad), unused = lax.scan(
        back_step, (query_start, jnp.zeros(kv_local.shape, jnp.float32)), (kv_blocks, sources)
    )
    query_grad_low = (
        rotate_back(query_grad.reshape(token_rows, head_count, HD), cosine, sine)
        .reshape(token_rows, head_count * HD)
        .astype(jnp.bfloat16)
    )
    key_grad_low = (
        rotate_back(kv_grad[:, : kv_heads * HD].reshape(token_rows, kv_heads, HD), cosine, sine)
        .reshape(token_rows, kv_heads * HD)
        .astype(jnp.bfloat16)
    )
    value_grad_low = kv_grad[:, kv_heads * HD :].astype(jnp.bfloat16)
    normed_one_grad = lax.psum(
        (
            project_back(query_grad_low, query_w)
            + project_back(key_grad_low, key_w)
            + project_back(value_grad_low, value_w)
        ).astype(jnp.bfloat16),
        "tp",
    ).astype(jnp.float32)
    query_w_grad = weight_grad(normed_low, query_grad_low)
    key_w_grad = weight_grad(normed_low, key_grad_low)
    value_w_grad = weight_grad(normed_low, value_grad_low)
    norm_back_one, gain_one_grad = rms_norm_back(normed_one_grad, gain_one_float, unit_one, inv_one)
    input_grad = (middle_grad + norm_back_one).astype(jnp.bfloat16)
    summed = (
        lax.psum_scatter(
            gain_one_grad.astype(jnp.bfloat16), ("fsdp", "ctx"), scatter_dimension=0, tiled=True
        ).astype(jnp.float32),
        lax.psum_scatter(
            query_w_grad.astype(jnp.bfloat16), ("fsdp", "ctx"), scatter_dimension=0, tiled=True
        ).astype(jnp.float32),
        lax.psum_scatter(
            key_w_grad.astype(jnp.bfloat16), ("fsdp", "ctx"), scatter_dimension=0, tiled=True
        ).astype(jnp.float32),
        lax.psum_scatter(
            value_w_grad.astype(jnp.bfloat16), ("fsdp", "ctx"), scatter_dimension=0, tiled=True
        ).astype(jnp.float32),
        lax.psum_scatter(
            out_w_grad.astype(jnp.bfloat16), ("fsdp", "ctx"), scatter_dimension=1, tiled=True
        ).astype(jnp.float32),
        lax.psum_scatter(
            gain_two_grad.astype(jnp.bfloat16), ("fsdp", "ctx"), scatter_dimension=0, tiled=True
        ).astype(jnp.float32),
        lax.psum_scatter(
            gate_w_grad.astype(jnp.bfloat16), ("fsdp", "ctx"), scatter_dimension=0, tiled=True
        ).astype(jnp.float32),
        lax.psum_scatter(
            up_w_grad.astype(jnp.bfloat16), ("fsdp", "ctx"), scatter_dimension=0, tiled=True
        ).astype(jnp.float32),
        lax.psum_scatter(
            down_w_grad.astype(jnp.bfloat16), ("fsdp", "ctx"), scatter_dimension=1, tiled=True
        ).astype(jnp.float32),
    )
    return (output, input_grad) + tuple(summed)


MESH = pl.DeviceIdType.MESH
BF = jnp.bfloat16
F32 = jnp.float32


def dotg(left_side, right_side, left_dim, right_dim):
    return lax.dot_general(
        left_side,
        right_side,
        (((left_dim,), (right_dim,)), ((), ())),
        preferred_element_type=F32,
    )


def remote(src, dst, send_sem, recv_sem, device):
    return pltpu.make_async_remote_copy(
        src_ref=src,
        dst_ref=dst,
        send_sem=send_sem,
        recv_sem=recv_sem,
        device_id=device,
        device_id_type=MESH,
    )


class Place:
    def __init__(self):
        self.f = lax.axis_index("fsdp")
        self.c = lax.axis_index("ctx")
        self.z = lax.axis_index("tp")
        self.cx = self.c + 1 - 2 * lax.rem(self.c, 2)
        self.cy = lax.rem(self.c + 2, 4)
        self.cd = 3 - self.c
        self.of = 1 - self.f
        self.own = self.f * 4 + self.c
        self.sx = self.f * 4 + self.cx
        self.sy = self.f * 4 + self.cy
        self.sd = self.f * 4 + self.cd

    def at(self, f=None, c=None, z=None):
        return (
            self.f if f is None else f,
            self.c if c is None else c,
            self.z if z is None else z,
        )


def greet(devices):
    barrier = pltpu.get_barrier_semaphore()
    for device in devices:
        pl.semaphore_signal(barrier, inc=1, device_id=device, device_id_type=MESH)
    pl.semaphore_wait(barrier, len(devices))


def group_devices(me):
    return [
        me.at(c=me.cx),
        me.at(c=me.cy),
        me.at(c=me.cd),
        me.at(f=me.of),
        me.at(f=me.of, c=me.cx),
        me.at(f=me.of, c=me.cy),
        me.at(f=me.of, c=me.cd),
    ]


def column_devices(me):
    return [me.at(z=lax.rem(me.z + step, 4)) for step in (1, 2, 3)]


class Gather:
    def __init__(self, me, index, own, full, send, recv, local_sem):
        self.me, self.full, self.placed = me, full, own is None
        own = full.at[me.own] if own is None else own
        rows = full.shape[1]
        self.half_a = pl.ds(0, rows // 2)
        self.half_b = pl.ds(rows // 2, rows // 2)

        def copy(slot, src, dst, device):
            return remote(src, dst, send.at[index, slot], recv.at[index, slot], device)

        slot_own, slot_x, slot_y = full.at[me.own], full.at[me.sx], full.at[me.sy]
        to_x, to_y, to_core = me.at(c=me.cx), me.at(c=me.cy), me.at(f=me.of)
        diag_a = full.at[me.sd, self.half_a]
        diag_b = full.at[me.sd, self.half_b]
        self.own_x = copy(0, own, slot_own, to_x)
        self.own_y = copy(1, own, slot_own, to_y)
        self.own_core = copy(2, own, slot_own, to_core)
        self.pass_x = copy(3, full.at[me.sy, self.half_a], full.at[me.sy, self.half_a], to_x)
        self.pass_y = copy(4, full.at[me.sx, self.half_b], full.at[me.sx, self.half_b], to_y)
        self.core_x = copy(5, slot_x, slot_x, to_core)
        self.core_y = copy(6, slot_y, slot_y, to_core)
        self.core_a = copy(7, diag_a, diag_a, to_core)
        self.core_b = copy(8, diag_b, diag_b, to_core)
        other = me.of * 4
        into = lambda slot, ref, device: copy(slot, ref, ref, device)
        self.in_x = into(0, slot_x, to_x)
        self.in_y = into(1, slot_y, to_y)
        self.in_a = into(3, diag_a, to_x)
        self.in_b = into(4, diag_b, to_y)
        self.in_core = [
            into(2, full.at[other + me.c], to_core),
            into(5, full.at[other + me.cx], to_core),
            into(6, full.at[other + me.cy], to_core),
            into(7, full.at[other + me.cd, self.half_a], to_core),
            into(8, full.at[other + me.cd, self.half_b], to_core),
        ]
        self.keep = None if self.placed else pltpu.make_async_copy(own, slot_own, local_sem.at[index])

    def begin(self):
        self.own_x.start()
        self.own_y.start()
        self.own_core.start()
        if not self.placed:
            self.keep.start()

    def forward_a(self):
        self.in_y.wait_recv()
        self.pass_x.start()
        self.core_y.start()

    def forward_b(self):
        self.in_x.wait_recv()
        self.pass_y.start()
        self.core_x.start()

    def diagonal_a(self):
        self.in_a.wait_recv()
        self.core_a.start()

    def diagonal_b(self):
        self.in_b.wait_recv()
        self.core_b.start()

    def arrive(self):
        if not self.placed:
            self.keep.wait()
        for piece in self.in_core:
            piece.wait_recv()

    def settle(self):
        for piece in (
            self.own_x,
            self.own_y,
            self.own_core,
            self.pass_x,
            self.pass_y,
            self.core_x,
            self.core_y,
            self.core_a,
            self.core_b,
        ):
            piece.wait_send()


class LineSum:
    def __init__(self, me, part, outer_in, inner_in, send, recv):
        self.me, self.part = me, part
        self.outer_in, self.inner_in = outer_in, inner_in
        self.send, self.recv = send, recv
        z = me.z
        self.is_mid = (z == 1) | (z == 2)
        self.is_end = (z == 0) | (z == 3)
        self.mid_of_end = 1 + z // 3
        self.outer_of_mid = 3 * (z - 1)

    def end_copies(self):
        me, part = self.me, self.part
        mid = self.mid_of_end
        to_mid = me.at(z=mid)
        owners = (3 - me.z, 3 - mid, mid)
        return [
            remote(
                part.at[owner],
                self.outer_in.at[slot],
                self.send.at[slot],
                self.recv.at[slot],
                to_mid,
            )
            for slot, owner in enumerate(owners)
        ]

    def mid_copies(self):
        me, part = self.me, self.part
        far_mid, outer = 3 - me.z, self.outer_of_mid
        far = 3 - outer
        to_mid, to_outer = me.at(z=far_mid), me.at(z=outer)
        return [
            remote(part.at[far], self.inner_in.at[0], self.send.at[0], self.recv.at[3], to_mid),
            remote(part.at[far_mid], self.inner_in.at[1], self.send.at[1], self.recv.at[4], to_mid),
            remote(part.at[outer], self.inner_in.at[0], self.send.at[2], self.recv.at[3], to_outer),
        ]

    def wait_in(self, slot, buffer):
        remote(buffer, buffer, self.send.at[0], self.recv.at[slot], self.me.at(z=3 - self.me.z)).wait_recv()

    def add(self, owner, buffer):
        self.part[owner] = (self.part[owner].astype(F32) + buffer[...].astype(F32)).astype(BF)

    def begin(self):
        @pl.when(self.is_end)
        def _():
            for piece in self.end_copies():
                piece.start()

    def step_one(self):
        @pl.when(self.is_mid)
        def _():
            far = 3 - self.outer_of_mid
            self.wait_in(0, self.outer_in.at[0])
            self.add(far, self.outer_in.at[0])
            self.mid_copies()[0].start()

    def step_two(self):
        @pl.when(self.is_mid)
        def _():
            copies = self.mid_copies()
            self.wait_in(1, self.outer_in.at[1])
            self.add(3 - self.me.z, self.outer_in.at[1])
            copies[1].start()

    def step_three(self):
        @pl.when(self.is_mid)
        def _():
            self.wait_in(3, self.inner_in.at[0])
            self.add(self.outer_of_mid, self.inner_in.at[0])
            self.mid_copies()[2].start()

    def finish(self, total):
        me = self.me

        @pl.when(self.is_mid)
        def _():
            self.wait_in(2, self.outer_in.at[2])
            self.wait_in(4, self.inner_in.at[1])
            total[...] = (
                self.part[me.z].astype(F32)
                + self.outer_in[2].astype(F32)
                + self.inner_in[1].astype(F32)
            )
            for piece in self.mid_copies():
                piece.wait_send()

        @pl.when(self.is_end)
        def _():
            self.wait_in(3, self.inner_in.at[0])
            total[...] = self.part[me.z].astype(F32) + self.inner_in[0].astype(F32)
            for piece in self.end_copies():
                piece.wait_send()


class LineGather:
    def __init__(self, me, blocks, send, recv):
        self.me, self.blocks, self.send, self.recv = me, blocks, send, recv
        z = me.z
        self.is_mid = (z == 1) | (z == 2)
        self.is_end = (z == 0) | (z == 3)
        self.mid_of_end = 1 + z // 3
        self.outer_of_mid = 3 * (z - 1)

    def copy(self, owner, slot, z):
        ref = self.blocks.at[owner]
        return remote(ref, ref, self.send.at[slot], self.recv.at[owner], self.me.at(z=z))

    def wait_in(self, owner):
        ref = self.blocks.at[owner]
        remote(ref, ref, self.send.at[0], self.recv.at[owner], self.me.at(z=3 - self.me.z)).wait_recv()

    def begin(self):
        me = self.me

        @pl.when(self.is_end)
        def _():
            self.copy(me.z, 0, self.mid_of_end).start()

        @pl.when(self.is_mid)
        def _():
            self.copy(me.z, 0, self.outer_of_mid).start()
            self.copy(me.z, 1, 3 - me.z).start()

    def step_one(self):
        me = self.me

        @pl.when(self.is_mid)
        def _():
            self.wait_in(self.outer_of_mid)
            self.copy(self.outer_of_mid, 2, 3 - me.z).start()

    def step_two(self):
        me = self.me

        @pl.when(self.is_mid)
        def _():
            self.wait_in(3 - me.z)
            self.copy(3 - me.z, 3, self.outer_of_mid).start()

    def step_three(self):
        @pl.when(self.is_mid)
        def _():
            far = 3 - self.outer_of_mid
            self.wait_in(far)
            self.copy(far, 4, self.outer_of_mid).start()

    def finish(self):
        me = self.me

        @pl.when(self.is_mid)
        def _():
            self.copy(me.z, 0, self.outer_of_mid).wait_send()
            self.copy(me.z, 1, 3 - me.z).wait_send()
            self.copy(self.outer_of_mid, 2, 3 - me.z).wait_send()
            self.copy(3 - me.z, 3, self.outer_of_mid).wait_send()
            self.copy(3 - self.outer_of_mid, 4, self.outer_of_mid).wait_send()

        @pl.when(self.is_end)
        def _():
            mid = self.mid_of_end
            self.wait_in(mid)
            self.wait_in(3 - mid)
            self.wait_in(3 - me.z)
            self.copy(me.z, 0, mid).wait_send()


def row_of(gains_ref, which):
    return jnp.concatenate([gains_ref[shard, which : which + 1, :] for shard in range(8)], axis=-1)


def swap_halves(rows):
    lane = lax.broadcasted_iota(jnp.int32, rows.shape, 1)
    return jnp.where(
        lax.rem(lane, HD) < HD // 2, pltpu.roll(rows, 96, 1), pltpu.roll(rows, 32, 1)
    )


class Scatter:
    def __init__(self, me, index, last, width, x_of, y_of, chips, refs):
        self.me, self.index, self.last, self.width = me, index, last, width
        self.x_of, self.y_of, self.chips = x_of, y_of, chips
        self.stage, self.core_in, self.diag_in, self.near_in = refs[:4]
        self.send, self.recv, self.credit = refs[4:]
        self.to_x, self.to_y, self.to_core = me.at(c=me.cx), me.at(c=me.cy), me.at(f=me.of)
        self.sent = []

    def copy(self, slot, src, dst, device):
        return remote(
            src, dst, self.send.at[self.index, slot], self.recv.at[self.index, slot], device
        )

    def lanes(self, ref):
        return ref.at[:, pl.ds(0, self.width)]

    def core_copy(self, role):
        return self.copy(
            role, self.stage(self.width, role), self.lanes(self.core_in.at[role]), self.to_core
        )

    def chunk(self, core, role):
        c = self.me.c
        high = lax.rem(c // 2 + role // 2, 2)
        low = lax.rem(lax.rem(c, 2) + lax.rem(role, 2), 2)
        return dotg(self.x_of(core * 4 + 2 * high + low), self.y_of(), 0, 0)

    def roles(self, body):
        def pair(step, carry):
            body(3 - step)
            body(1 - step)
            return carry

        lax.fori_loop(0, 2, pair, 0)

    def partner(self):
        def body(role):
            self.stage(self.width, role)[...] = self.chunk(self.me.of, role).astype(BF)
            if self.index > 0:
                pl.semaphore_wait(self.credit.at[role], 1)
            self.core_copy(role).start()

        self.roles(body)

    def own(self):
        def body(role):
            value = self.chunk(self.me.f, role)
            self.core_copy(role).wait_recv()
            chip = self.chips(role)
            chip[...] = (value + self.lanes(self.core_in.at[role])[...].astype(F32)).astype(BF)
            if not self.last:
                pl.semaphore_signal(
                    self.credit.at[role], inc=1, device_id=self.to_core, device_id_type=MESH
                )

        self.roles(body)
        for role in range(4):
            self.core_copy(role).wait_send()

    def near(self, role, half, slot):
        rows = pl.ds(half * 128, 128)
        side = role - 1
        device = self.to_x if role == 1 else self.to_y
        return self.copy(
            slot, self.chips(role).at[rows, :], self.near_in.at[side, rows, :], device
        )

    def diag(self, half):
        device = self.to_x if half == 0 else self.to_y
        return self.copy(
            4 + half,
            self.chips(3).at[pl.ds(half * 128, 128), :],
            self.lanes(self.diag_in.at[half]),
            device,
        )

    def push_diag(self):
        self.diag(0).start()
        self.diag(1).start()

    def push_near(self):
        self.near(1, 0, 6).start()
        self.near(2, 1, 7).start()

    def relay_a(self):
        first = pl.ds(0, 128)
        self.diag(0).wait_recv()
        rows = self.chips(2).at[first, :]
        rows[...] = (
            rows[...].astype(F32) + self.lanes(self.diag_in.at[0])[...].astype(F32)
        ).astype(BF)
        self.near(2, 0, 8).start()

    def relay_b(self):
        second = pl.ds(128, 128)
        self.diag(1).wait_recv()
        rows = self.chips(1).at[second, :]
        rows[...] = (
            rows[...].astype(F32) + self.lanes(self.diag_in.at[1])[...].astype(F32)
        ).astype(BF)
        self.near(1, 1, 9).start()

    def collect(self, buffer, sem):
        for role, half, slot in ((1, 0, 6), (2, 1, 7), (2, 0, 8), (1, 1, 9)):
            self.near(role, half, slot).wait_recv()
        for side in range(2):
            pltpu.make_async_copy(
                self.near_in.at[side], self.lanes(buffer.at[side]), sem.at[side]
            ).start()

    def collected(self, buffer, sem):
        for side in range(2):
            pltpu.make_async_copy(
                self.near_in.at[side], self.lanes(buffer.at[side]), sem.at[side]
            ).wait()

    def settle(self):
        for half in range(2):
            self.diag(half).wait_send()
        for role, half, slot in ((1, 0, 6), (2, 1, 7), (2, 0, 8), (1, 1, 9)):
            self.near(role, half, slot).wait_send()


def norm_back(gradient, rows_in, gain):
    inv = lax.rsqrt(jnp.mean(rows_in * rows_in, axis=-1, keepdims=True) + EPSILON)
    unit = rows_in * inv
    scaled = gradient * gain
    back = inv * (scaled - unit * jnp.mean(scaled * unit, axis=-1, keepdims=True))
    return back, jnp.sum(gradient * unit, axis=0, keepdims=True)


def layer_kernel(
    tok_h,
    gains_in,
    w_query_in,
    w_key_in,
    w_value_in,
    out_h,
    gate_h,
    up_h,
    down_h,
    cot_h,
    pos_in,
    seg_in,
    freq,
    o_result,
    o_input,
    o_gain_one,
    o_gain_two,
    o_query,
    o_key,
    o_value,
    o_out,
    o_gate,
    o_up,
    o_down,
    near_down,
    near_gate,
    near_up,
    near_out,
    near_qkv,
    n_one_h,
    own_gains,
    own_marks,
    gains,
    marks,
    tok,
    w_gate,
    w_up,
    w_down,
    w_out,
    w_qkv,
    cot,
    n_two,
    hid,
    gate_g,
    up_g,
    core_in,
    diag_in,
    diag_low,
    chip_out,
    chip_qkv,
    sum_stage,
    turn_stage,
    part,
    outer_in,
    inner_in,
    outer_two,
    inner_two,
    mlow,
    total,
    own_out,
    mid,
    mid_g,
    q_rot,
    bias,
    lse,
    kv,
    att,
    rope,
    do_rows,
    keys,
    vals_t,
    vals,
    keys_t,
    key_acc,
    val_acc,
    kv_send_buf,
    kv_in,
    d_qkv,
    vec,
    vec_in,
    vec_out,
    vec_near,
    g_send,
    g_recv,
    g_local,
    small_send,
    small_recv,
    first_send,
    first_recv,
    load_sem,
    sum_send,
    sum_recv,
    all_send,
    all_recv,
    rs_send,
    rs_recv,
    credit,
    kv_send,
    kv_recv,
    vec_send,
    vec_recv,
    fin_sem,
    put_sem,
    own_sem,
):
    me = Place()
    group = group_devices(me)
    hidden = hid.shape[1]

    rows_of = [pl.ds(g * 256, 256) for g in range(2)]
    load_tok = pltpu.make_async_copy(tok_h, tok, load_sem.at[0])
    load_cot = pltpu.make_async_copy(cot_h, cot, load_sem.at[1])
    save_one = pltpu.make_async_copy(mlow, n_one_h, load_sem.at[2])
    load_one = pltpu.make_async_copy(n_one_h, mlow, load_sem.at[3])
    load_tok.start()
    load_cot.start()

    w_qkv[me.own, :, 0:512] = w_query_in[...]
    turned = jnp.concatenate([w_key_in[...], w_value_in[...]], axis=0).astype(F32)
    w_qkv[me.own, :, 512:640] = jnp.transpose(turned).astype(BF)
    own_gains[0:2, :] = gains_in[...].astype(F32)
    own_gains[2:8, :] = jnp.zeros((6, 256), F32)
    own_marks[0:1, :] = pos_in[...]
    own_marks[1:2, :] = seg_in[...]
    own_marks[2:8, :] = jnp.zeros((6, 512), jnp.int32)
    greet(group + column_devices(me))

    qkv = Gather(me, 0, None, w_qkv, g_send, g_recv, g_local)
    out = Gather(me, 1, out_h, w_out, g_send, g_recv, g_local)
    gate = Gather(me, 2, gate_h, w_gate, g_send, g_recv, g_local)
    up = Gather(me, 3, up_h, w_up, g_send, g_recv, g_local)
    down = Gather(me, 4, down_h, w_down, g_send, g_recv, g_local)

    sources = [me.sx, me.sy, me.sd, me.of * 4 + me.c, me.of * 4 + me.cx, me.of * 4 + me.cy, me.of * 4 + me.cd]

    def small_copies(gain_slots, mark_slots):
        return [
            remote(own_gains, gains.at[spot], small_send.at[slot], small_recv.at[slot], group[slot])
            for slot, spot in enumerate(gain_slots)
        ] + [
            remote(
                own_marks, marks.at[spot], small_send.at[7 + slot], small_recv.at[7 + slot], group[slot]
            )
            for slot, spot in enumerate(mark_slots)
        ]

    small = small_copies([me.own] * 7, [me.c] * 3)

    def small_begin():
        for piece in small:
            piece.start()
        gains[me.own] = own_gains[...]
        marks[me.c] = own_marks[...]

    def small_finish():
        for piece in small_copies(sources, (me.cx, me.cy, me.cd)):
            piece.wait_recv()

    def first_norm():
        load_tok.wait()
        gain_one = row_of(gains, 0)

        def body(step, carry):
            values = tok[pl.ds(pl.multiple_of(step * 64, 64), 64), :].astype(F32)
            inv = lax.rsqrt(jnp.mean(values * values, axis=-1, keepdims=True) + EPSILON)
            mlow[step // 4, lax.rem(step, 4)] = (values * inv * gain_one).astype(BF)
            return carry

        lax.fori_loop(0, 8, body, 0)
        save_one.start()

    def make_rope():
        lane = lax.broadcasted_iota(jnp.int32, (128, 128), 1)
        low_half = lax.rem(lane, HD) < HD // 2
        for step in range(4):
            rows = slice(step * 128, (step + 1) * 128)
            places = own_marks[0:1, rows].astype(F32)
            angles = jnp.transpose(jnp.broadcast_to(places, (128, 128))) * freq[...]
            sine = jnp.sin(angles)
            rope[rows, :128] = jnp.cos(angles)
            rope[rows, 128:] = jnp.where(low_half, -sine, sine)

    def make_bias(g):
        own_rows = own_marks[:, g * 256 : (g + 1) * 256].astype(F32)
        for source in range(4):
            key_rows = marks[source, :, g * 256 : (g + 1) * 256].astype(F32)
            key_pos = jnp.transpose(jnp.broadcast_to(key_rows[0:1, :], (128, 256)))
            key_seg = jnp.transpose(jnp.broadcast_to(key_rows[1:2, :], (128, 256)))
            for side in range(2):
                lanes = slice(side * 128, (side + 1) * 128)
                seen = (key_seg == own_rows[1:2, lanes]) & (key_pos <= own_rows[0:1, lanes])
                bias[g, source * 256 : (source + 1) * 256, lanes] = jnp.where(
                    seen, 0.0, MASKED_SCORE
                ).astype(BF)

    lane_pair = lax.broadcasted_iota(jnp.int32, (256, 128), 1)

    def project_in(first, width):
        total_rows = None
        for shard in range(8):
            term = dotg(
                mlow[:, :, :, shard * 256 : (shard + 1) * 256].reshape(512, 256),
                w_qkv[shard, :, first : first + width],
                1,
                0,
            )
            total_rows = term if total_rows is None else total_rows + term
        return total_rows

    def first_copies(places):
        return [
            remote(kv.at[place], kv.at[place], first_send.at[slot], first_recv.at[slot], group[slot])
            for slot, place in enumerate(places)
        ]

    def project_kv():
        rows = project_in(512, 128)
        is_key = lax.broadcasted_iota(jnp.int32, (512, 128), 1) < HD
        cos_rows = jnp.where(is_key, rope[:, :128], 1.0)
        sin_rows = jnp.where(is_key, rope[:, 128:], 0.0)
        kv[me.c] = (rows * cos_rows + swap_halves(rows) * sin_rows).astype(BF)
        for piece in first_copies([me.c] * 3):
            piece.start()

    def project_q(half):
        rows_all = project_in(half * 256, 256)
        for inner in range(2):
            pair = half * 2 + inner
            rows = rows_all[:, inner * 128 : (inner + 1) * 128]
            rot = (rows * rope[:, :128] + swap_halves(rows) * rope[:, 128:]).astype(BF)
            rot = rot * jnp.bfloat16(HD ** (-0.5))
            q_rot[:, pair * 128 : (pair + 1) * 128] = rot

    def kv_arrive():
        for piece in first_copies((me.cx, me.cy, me.cd)):
            piece.wait_recv()
        for g in range(2):
            for source in range(4):
                pairs = kv[source, g * 256 : (g + 1) * 256, :].astype(F32)
                rows = slice(source * 256, (source + 1) * 256)
                keys[g, rows, :] = jnp.where(
                    lane_pair < HD, pairs, pltpu.roll(pairs, HD, 1)
                ).astype(BF)
                vals_t[g, :, rows] = jnp.transpose(pairs)[HD:, :].astype(BF)

    def one_head(pair_rows, odd):
        kept = lane_pair >= HD if odd else lane_pair < HD
        return jnp.where(kept, pair_rows, jnp.zeros_like(pair_rows))

    def attend(step):
        g = step // 4
        pair = step - g * 4
        halves = []
        own = pl.ds(pl.multiple_of(g * 256, 256), 256)
        lanes = pl.ds(pl.multiple_of(pair * 128, 128), 128)
        queries = q_rot[own, lanes]
        for odd in range(2):
            head = step * 2 + odd
            scores = dotg(keys[g], one_head(queries, odd), 1, 1) + bias[g].astype(F32)
            top = jnp.max(scores, axis=0, keepdims=True)
            weights = jnp.exp(scores - top)
            norm = jnp.sum(weights, axis=0, keepdims=True)
            mixed = dotg(vals_t[g], weights.astype(BF), 1, 0)
            halves.append(mixed / norm)
            lse[head] = top + jnp.log(norm)
        rows = jnp.transpose(jnp.concatenate(halves, axis=0))
        att[own, lanes] = rows.astype(BF)

    def project_out(g):
        def body(shard, carry):
            part[g, :, :, pl.ds(pl.multiple_of(shard * 256, 256), 256)] = (
                dotg(att[rows_of[g], :], w_out[shard], 1, 0).astype(BF).reshape(4, 64, 256)
            )
            return carry

        lax.fori_loop(0, 8, body, 0)

    def second_norm(g):
        sum_att[g].finish(total)
        own = pl.ds(pl.multiple_of(g * 256 + me.z * 64, 64), 64)
        mid_rows = tok[own, :].astype(F32) + total[...]
        mid[g] = mid_rows
        inv = lax.rsqrt(jnp.mean(mid_rows * mid_rows, axis=-1, keepdims=True) + EPSILON)
        n_two[g, me.z] = (mid_rows * inv * row_of(gains, 1)).astype(BF)
        spread_two[g].begin()

    def looped(body, count, hooks):
        def step(i, carry):
            for spot, actions in hooks:

                @pl.when(i == spot)
                def _():
                    for action, *values in actions:
                        action(*values)

            body(i)
            return carry

        lax.fori_loop(0, count, step, 0)

    tile_count = (hidden + 255) // 256

    def feed(step):
        g = step // tile_count
        n = step - g * tile_count
        rows = pl.ds(pl.multiple_of(g * 256, 256), 256)
        lanes = pl.ds(pl.multiple_of(jnp.minimum(n * 256, hidden - 256), 128), 256)
        normed = n_two[g].reshape(256, 2048)
        gate = dotg(normed, w_gate[:, :, lanes].reshape(2048, 256), 1, 0)
        up = dotg(normed, w_up[:, :, lanes].reshape(2048, 256), 1, 0)
        hidden_grad = None
        for shard in range(8):
            term = dotg(
                cot[rows, shard * 256 : (shard + 1) * 256], w_down[shard, lanes, :], 1, 1
            )
            hidden_grad = term if hidden_grad is None else hidden_grad + term
        sig = jax.nn.sigmoid(gate)
        silu = gate * sig
        hid[rows, lanes] = (silu * up).astype(BF)
        up_g[rows, lanes] = (hidden_grad * silu).astype(BF)
        gate_g[rows, lanes] = (
            hidden_grad * up * sig * (1.0 + gate * (1.0 - sig))
        ).astype(BF)

    def feed_back(g):
        def body(shard, carry):
            term = dotg(gate_g[rows_of[g], :], w_gate[shard], 1, 1) + dotg(
                up_g[rows_of[g], :], w_up[shard], 1, 1
            )
            part[g, :, :, pl.ds(pl.multiple_of(shard * 256, 256), 256)] = term.astype(BF).reshape(
                4, 64, 256
            )
            return carry

        lax.fori_loop(0, 8, body, 0)

    part_two = n_two

    def feed_out(g):
        def body(shard, carry):
            term = dotg(hid[rows_of[g], :], w_down[shard], 1, 0)
            part_two[g, :, :, pl.ds(pl.multiple_of(shard * 256, 256), 256)] = term.astype(
                BF
            ).reshape(4, 64, 256)
            return carry

        lax.fori_loop(0, 8, body, 0)

    def line_sum(slot, part_ref, outer, inner):
        return LineSum(me, part_ref, outer, inner, sum_send.at[slot], sum_recv.at[slot])

    sum_two = [line_sum(g, part.at[g], outer_in.at[g], inner_in.at[g]) for g in range(2)]
    sum_one = [line_sum(2 + g, part.at[g], outer_in.at[g], inner_in.at[g]) for g in range(2)]

    sum_out = [
        line_sum(4 + g, part_two.at[g], outer_two.at[g], inner_two.at[g]) for g in range(2)
    ]
    sum_att = [line_sum(6 + g, part.at[g], outer_in.at[g], inner_in.at[g]) for g in range(2)]
    spread_two = [LineGather(me, n_two.at[g], all_send.at[6 + g], all_recv.at[6 + g]) for g in range(2)]
    spread_mid = [LineGather(me, mlow.at[g], all_send.at[g], all_recv.at[g]) for g in range(2)]
    spread_in = [LineGather(me, o_input.at[g], all_send.at[2 + g], all_recv.at[2 + g]) for g in range(2)]
    spread_out = [LineGather(me, o_result.at[g], all_send.at[4 + g], all_recv.at[4 + g]) for g in range(2)]

    def middle_back(g):
        sum_two[g].finish(total)
        own = pl.ds(pl.multiple_of(g * 256 + me.z * 64, 64), 64)
        back, gain_grad = norm_back(total[...], mid[g], row_of(gains, 1))
        if g == 0:
            vec[1:2, :] = gain_grad
        else:
            vec[1:2, :] += gain_grad
        grad = cot[own, :].astype(F32) + back
        mid_g[g] = grad
        mlow[g, me.z] = grad.astype(BF)
        spread_mid[g].begin()

    def put_own(g, ref, slot):
        copy = pltpu.make_async_copy(own_out, ref.at[g, me.z], own_sem.at[slot])
        copy.start()
        copy.wait()

    def input_back(g):
        sum_one[g].finish(total)
        own = pl.ds(pl.multiple_of(g * 256 + me.z * 64, 64), 64)
        back, gain_grad = norm_back(total[...], tok[own, :].astype(F32), row_of(gains, 0))
        if g == 0:
            vec[0:1, :] = gain_grad
        else:
            vec[0:1, :] += gain_grad
        own_out[...] = (mid_g[g] + back).astype(BF)
        put_own(g, o_input, 0)
        spread_in[g].begin()

    def result_rows(g):
        sum_out[g].finish(total)
        own_out[...] = (mid[g] + total[...]).astype(BF)
        put_own(g, o_result, 1)
        spread_out[g].begin()

    wide = lambda ref: (lambda shard: ref[:, pl.ds(pl.multiple_of(shard * 256, 256), 256)])

    def blocks_of(ref):
        return lambda shard: ref[
            :, :, :, pl.ds(pl.multiple_of(shard * 256, 256), 256)
        ].reshape(512, 256)

    def stage(width, slot):
        if width > 640:
            return w_up.at[4 + slot]
        first = lax.rem(slot, 2) * 640
        if not isinstance(slot, int):
            first = pl.multiple_of(first, 128)
        return w_up.at[4 + slot // 2, :, pl.ds(first, width)]

    landing = w_up.at[pl.ds(6, 2)]

    def scatter(index, width, x_of, y_of, chips, near):
        landed = diag_in.at[index] if index < 3 else diag_low.at[index - 3]
        refs = (stage, core_in, landed, near, rs_send, rs_recv, credit)
        return Scatter(me, index, index == 4, width, x_of, y_of, chips, refs)

    rs_down = scatter(
        0, hidden, wide(cot), lambda: hid[...], lambda role: w_gate.at[4 + role], near_down
    )
    rs_gate = scatter(
        1, hidden, blocks_of(n_two), lambda: gate_g[...], lambda role: w_gate.at[role], near_gate
    )
    rs_up = scatter(
        2, hidden, blocks_of(n_two), lambda: up_g[...], lambda role: w_up.at[role], near_up
    )
    rs_out = scatter(3, 512, blocks_of(mlow), lambda: att[...], lambda role: chip_out.at[role], near_out)
    rs_qkv = scatter(
        4,
        640,
        blocks_of(mlow),
        lambda: d_qkv[...],
        lambda role: chip_qkv.at[role],
        near_qkv,
    )

    def finish_rows(job, outs):
        job.collected(landing, fin_sem)
        width = job.width
        pending = [None, None]
        for step in range(4):
            slot = step % 2
            rows = slice(step * 64, (step + 1) * 64)
            if pending[slot] is not None:
                for piece in pending[slot]:
                    piece.wait()
            sum_stage[slot, :, :width] = (
                job.chips(0)[rows, :].astype(F32)
                + landing[0, rows, :width].astype(F32)
                + landing[1, rows, :width].astype(F32)
            )
            pending[slot] = [
                pltpu.make_async_copy(
                    sum_stage.at[slot, :, pl.ds(first, size)],
                    ref.at[pl.ds(step * 64, 64), :],
                    put_sem.at[slot, number],
                )
                for number, (ref, first, size) in enumerate(outs)
            ]
            for piece in pending[slot]:
                piece.start()
        for slot in range(2):
            for piece in pending[slot]:
                piece.wait()

    def finish_qkv(job):
        finish_rows(job, [(o_query, 0, 512)])
        lanes = slice(512, 640)
        turn_stage[0] = jnp.transpose(
            job.chips(0)[:, lanes].astype(F32)
            + landing[0, :, lanes].astype(F32)
            + landing[1, :, lanes].astype(F32)
        )
        copies = [
            pltpu.make_async_copy(
                turn_stage.at[0, pl.ds(first, HD), :], ref, put_sem.at[0, number]
            )
            for number, (first, ref) in enumerate(((0, o_key), (HD, o_value)))
        ]
        for piece in copies:
            piece.start()
        for piece in copies:
            piece.wait()

    def finish_turned(job, ref):
        job.collected(landing, fin_sem)

        def put(step, slot):
            rows = pl.ds(pl.multiple_of(step * 128, 128), 128)
            return pltpu.make_async_copy(turn_stage.at[slot], ref.at[rows, :], put_sem.at[slot, 0])

        def body(step, carry):
            slot = lax.rem(step, 2)
            lanes = pl.ds(pl.multiple_of(step * 128, 128), 128)

            @pl.when(step >= 2)
            def _():
                put(step, slot).wait()

            turn_stage[slot] = jnp.transpose(
                job.chips(0)[:, lanes].astype(F32)
                + landing[0, :, lanes].astype(F32)
                + landing[1, :, lanes].astype(F32)
            )
            put(step, slot).start()
            return carry

        lax.fori_loop(0, job.width // 128, body, 0)
        for slot in range(2):
            put(slot, slot).wait()

    def out_back(g):
        grad = None
        for shard in range(8):
            lanes = slice(shard * 256, (shard + 1) * 256)
            term = dotg(mlow[g, :, :, lanes].reshape(256, 256), w_out[shard], 1, 1)
            grad = term if grad is None else grad + term
        do_rows[...] = grad.astype(BF)
        for source in range(4):
            pairs = kv[source, rows_of[g], :].astype(F32)
            turned = pltpu.roll(pairs, HD, 1)
            rows = slice(source * 256, (source + 1) * 256)
            vals[rows, :] = jnp.where(lane_pair < HD, turned, pairs).astype(BF)
            keys_t[:, rows] = jnp.transpose(pairs)[:HD, :].astype(BF)
        key_acc[...] = jnp.zeros_like(key_acc)
        val_acc[...] = jnp.zeros_like(val_acc)

    def attend_back(step):
        g = step // 4
        pair = step - g * 4
        own = pl.ds(pl.multiple_of(g * 256, 256), 256)
        halves = []
        lanes = pl.ds(pl.multiple_of(pair * 128, 128), 128)
        queries, grads = q_rot[own, lanes], do_rows[:, lanes]
        for odd in range(2):
            query, grad = one_head(queries, odd), one_head(grads, odd)
            scores = dotg(keys[g], query, 1, 1) + bias[g].astype(F32)
            probs = jnp.exp(scores - lse[step * 2 + odd])
            prob_grad = dotg(vals[...], grad, 1, 1)
            delta = jnp.sum(probs * prob_grad, axis=0, keepdims=True)
            score_grad = (probs * (prob_grad - delta)).astype(BF)
            val_acc[...] += dotg(probs.astype(BF), grad, 1, 0)
            key_acc[...] += dotg(score_grad, query, 1, 0)
            halves.append(dotg(keys_t[...], score_grad, 1, 0))
        rows = jnp.transpose(jnp.concatenate(halves, axis=0)) * (HD ** (-0.5))
        rows = rows * rope[own, :128] - swap_halves(rows) * rope[own, 128:]
        d_qkv[own, lanes] = rows.astype(BF)

    def kv_copies(g):
        return [
            remote(
                kv_send_buf.at[g, column],
                kv_in.at[g, slot],
                kv_send.at[g, slot],
                kv_recv.at[g, slot],
                group[slot],
            )
            for slot, column in enumerate((me.cx, me.cy, me.cd))
        ]

    def kv_begin(g):
        for block in range(4):
            rows = slice(block * 256, (block + 1) * 256)
            key_rows, val_rows = key_acc[rows, :], val_acc[rows, :]
            joined = jnp.where(
                lane_pair < HD,
                key_rows + pltpu.roll(key_rows, HD, 1),
                val_rows + pltpu.roll(val_rows, HD, 1),
            )
            kv_send_buf[g, block] = joined.astype(BF)
        for piece in kv_copies(g):
            piece.start()

    def kv_finish(g):
        rows = kv_send_buf[g, me.c].astype(F32)
        for slot, piece in enumerate(kv_copies(g)):
            piece.wait_recv()
            rows = rows + kv_in[g, slot].astype(F32)
        cos_rows = jnp.where(lane_pair < HD, rope[rows_of[g], :128], 1.0)
        sin_rows = jnp.where(lane_pair < HD, rope[rows_of[g], 128:], 0.0)
        rows = rows * cos_rows - swap_halves(rows) * sin_rows
        d_qkv[rows_of[g], 512:640] = rows.astype(BF)

    def project_back_rows(g):
        def body(shard, carry):
            term = dotg(d_qkv[rows_of[g], :], w_qkv[shard], 1, 1)
            part[g, :, :, pl.ds(pl.multiple_of(shard * 256, 256), 256)] = term.astype(BF).reshape(
                4, 64, 256
            )
            return carry

        lax.fori_loop(0, 8, body, 0)

    line = column_devices(me)

    def vec_line():
        return [
            remote(vec_out, vec_in.at[slot], vec_send.at[slot], vec_recv.at[slot], device)
            for slot, device in enumerate(line)
        ]

    targets = [me.sx, me.sy, me.sd, me.of * 4 + me.c, me.of * 4 + me.cx, me.of * 4 + me.cy, me.of * 4 + me.cd]

    def vec_group():
        return [
            remote(
                vec_in.at[3, target],
                vec_near.at[slot],
                vec_send.at[3 + slot],
                vec_recv.at[3 + slot],
                device,
            )
            for slot, (target, device) in enumerate(zip(targets, group))
        ]

    def vec_begin():
        for shard in range(8):
            for which in range(2):
                for half in range(2):
                    first = shard * 256 + half * 128
                    vec_out[shard, 2 * which + half : 2 * which + half + 1, :] = vec[
                        which : which + 1, first : first + 128
                    ]
            vec_out[shard, 4:8, :] = jnp.zeros((4, 128), F32)
        for piece in vec_line():
            piece.start()

    def vec_middle():
        for piece in vec_line():
            piece.wait_recv()
        vec_in[3] = vec_out[...] + vec_in[0] + vec_in[1] + vec_in[2]
        for piece in vec_group():
            piece.start()

    def vec_finish():
        rows = vec_in[3, me.own]
        for slot, piece in enumerate(vec_group()):
            piece.wait_recv()
            rows = rows + vec_near[slot]
        o_gain_one[...] = rows[0:2, :]
        o_gain_two[...] = rows[2:4, :]

    def settle_weights():
        for piece in (qkv, out, gate, up, down):
            piece.settle()

    def settle():
        for spread in spread_in + spread_out:
            spread.finish()
        for job in (rs_down, rs_gate, rs_up, rs_out, rs_qkv):
            job.settle()
        for g in range(2):
            for piece in kv_copies(g):
                piece.wait_send()
        for piece in vec_line() + vec_group() + small + first_copies([me.c] * 3):
            piece.wait_send()

    order = (
        (small_begin,),
        (qkv.begin,),
        (make_rope,),
        (qkv.forward_a,),
        (qkv.forward_b,),
        (small_finish,),
        (first_norm,),
        (out.begin,),
        (qkv.diagonal_a,),
        (qkv.diagonal_b,),
        (qkv.arrive,),
        (project_kv,),
        (project_q, 0),
        (out.forward_a,),
        (make_bias, 0),
        (out.forward_b,),
        (project_q, 1),
        (save_one.wait,),
        (up.begin,),
        (kv_arrive,),
        (make_bias, 1),
        (down.begin,),
        (
            looped,
            attend,
            8,
            (
                (2, ((out.diagonal_a,), (out.diagonal_b,),)),
                (4, ((out.arrive,),)),
                (6, ((project_out, 0), (sum_att[0].begin,), (sum_att[0].step_one,),)),
            ),
        ),
        (project_out, 1),
        (load_cot.wait,),
        (gate.begin,),
        (sum_att[1].begin,),
        (sum_att[0].step_two,),
        (sum_att[0].step_three,),
        (second_norm, 0),
        (down.forward_a,),
        (down.forward_b,),
        (up.forward_a,),
        (sum_att[1].step_one,),
        (sum_att[1].step_two,),
        (spread_two[0].step_two,),
        (sum_att[1].step_three,),
        (second_norm, 1),
        (up.forward_b,),
        (down.diagonal_a,),
        (down.diagonal_b,),
        (spread_two[0].step_one,),
        (down.arrive,),
        (up.diagonal_a,),
        (gate.forward_a,),
        (spread_two[1].step_one,),
        (gate.forward_b,),
        (spread_two[0].step_three,),
        (up.diagonal_b,),
        (up.arrive,),
        (gate.diagonal_a,),
        (spread_two[1].step_two,),
        (gate.diagonal_b,),
        (spread_two[0].finish,),
        (gate.arrive,),
        (settle_weights,),
        (
            looped,
            feed,
            2 * tile_count,
            (
                (3, ((spread_two[1].step_three,),)),
                (6, ((feed_back, 0), (sum_two[0].begin,), (spread_two[1].finish,),)),
            ),
        ),
        (feed_back, 1),
        (sum_two[0].step_one,),
        (sum_two[0].step_two,),
        (sum_two[1].begin,),
        (rs_down.partner,),
        (sum_two[0].step_three,),
        (rs_down.own,),
        (rs_gate.partner,),
        (sum_two[1].step_one,),
        (middle_back, 0),
        (rs_gate.own,),
        (rs_up.partner,),
        (sum_two[1].step_three,),
        (sum_two[1].step_two,),
        (rs_up.own,),
        (spread_mid[0].step_one,),
        (spread_mid[0].step_two,),
        (rs_up.push_near,),
        (middle_back, 1),
        (rs_down.push_near,),
        (feed_out, 1),
        (spread_mid[1].step_one,),
        (rs_gate.push_near,),
        (feed_out, 0),
        (spread_mid[0].step_three,),
        (sum_out[1].begin,),
        (sum_out[1].step_one,),
        (sum_out[0].begin,),
        (spread_mid[0].finish,),
        (out_back, 0),
        (rs_gate.push_diag,),
        (spread_mid[1].step_two,),
        (
            looped,
            attend_back,
            8,
            (
                (4, ((spread_mid[1].step_three,), (spread_mid[1].finish,), (kv_begin, 0), (sum_out[1].step_two,), (out_back, 1),)),
                (6, ((sum_out[1].step_three,), (rs_out.partner,), (sum_out[0].step_one,), (result_rows, 1), (rs_down.push_diag,),)),
            ),
        ),
        (kv_begin, 1),
        (rs_up.push_diag,),
        (kv_finish, 0),
        (project_back_rows, 0),
        (sum_out[0].step_three,),
        (sum_out[0].step_two,),
        (spread_out[1].step_two,),
        (sum_one[0].begin,),
        (rs_out.own,),
        (rs_out.push_diag,),
        (spread_out[1].step_one,),
        (kv_finish, 1),
        (project_back_rows, 1),
        (sum_one[1].begin,),
        (rs_gate.relay_a,),
        (result_rows, 0),
        (load_one.start,),
        (sum_one[0].step_one,),
        (spread_out[1].step_three,),
        (load_one.wait,),
        (rs_down.relay_a,),
        (sum_one[0].step_two,),
        (rs_qkv.partner,),
        (spread_out[0].step_two,),
        (sum_one[0].step_three,),
        (rs_out.relay_a,),
        (rs_up.relay_a,),
        (rs_up.relay_b,),
        (rs_down.relay_b,),
        (sum_one[1].step_one,),
        (rs_qkv.own,),
        (input_back, 0),
        (sum_one[1].step_two,),
        (sum_one[1].step_three,),
        (rs_qkv.push_diag,),
        (spread_in[0].step_two,),
        (spread_out[0].step_one,),
        (rs_gate.relay_b,),
        (input_back, 1),
        (rs_out.push_near,),
        (spread_in[0].step_one,),
        (rs_qkv.push_near,),
        (vec_begin,),
        (rs_down.collect, landing, fin_sem),
        (finish_turned, rs_down, o_down),
        (spread_out[0].step_three,),
        (rs_qkv.relay_a,),
        (spread_in[1].step_one,),
        (spread_in[1].step_two,),
        (rs_out.relay_b,),
        (rs_gate.collect, landing, fin_sem),
        (finish_rows, rs_gate, [(o_gate, 0, hidden)]),
        (rs_up.collect, landing, fin_sem),
        (finish_rows, rs_up, [(o_up, 0, hidden)]),
        (spread_in[0].step_three,),
        (rs_out.collect, landing, fin_sem),
        (finish_turned, rs_out, o_out),
        (rs_qkv.relay_b,),
        (spread_in[1].step_three,),
        (vec_middle,),
        (vec_finish,),
        (rs_qkv.collect, landing, fin_sem),
        (finish_qkv, rs_qkv),
        (settle,),
    )
    for action, *values in order:
        action(*values)


def run_layer(
    tokens, attn_gain, w_query, w_key, w_value, w_out, mlp_gain, w_gate, w_up, w_down, cotangent,
    positions, segments,
):
    shape = jax.ShapeDtypeStruct
    width = tokens.shape[1]
    hidden = w_gate.shape[1]
    vmem = pl.BlockSpec(memory_space=pltpu.VMEM)
    anywhere = pl.BlockSpec(memory_space=pl.ANY)
    dma = pltpu.SemaphoreType.DMA
    buffer = pltpu.VMEM
    half_size = HD // 2
    frequency = THETA_BASE ** (-np.arange(half_size, dtype=np.float32) / half_size)
    frequency = np.concatenate([frequency] * 4)[None, :].astype(np.float32)
    return pl.pallas_call(
        layer_kernel,
        name="decoder_layer",
        out_shape=(
            shape((2, 4, 64, width), BF),
            shape((2, 4, 64, width), BF),
            shape((2, 128), F32),
            shape((2, 128), F32),
            shape((256, 512), F32),
            shape((HD, 256), F32),
            shape((HD, 256), F32),
            shape((512, 256), F32),
            shape((256, hidden), F32),
            shape((256, hidden), F32),
            shape((hidden, 256), F32),
            shape((2, 256, hidden), BF),
            shape((2, 256, hidden), BF),
            shape((2, 256, hidden), BF),
            shape((2, 256, 512), BF),
            shape((2, 256, 640), BF),
            shape((2, 4, 64, width), BF),
        ),
        in_specs=[anywhere, vmem, vmem, vmem, vmem]
        + [anywhere] * 5
        + [vmem] * 3,
        out_specs=(anywhere,) * 2 + (vmem,) * 2 + (anywhere,) * 13,
        scratch_shapes=[
            buffer((8, 256), F32),
            buffer((8, 512), jnp.int32),
            buffer((8, 8, 256), F32),
            buffer((4, 8, 512), jnp.int32),
            buffer((512, width), BF),
            buffer((8, 256, hidden), BF),
            buffer((8, 256, hidden), BF),
            buffer((8, hidden, 256), BF),
            buffer((8, 512, 256), BF),
            buffer((8, 256, 640), BF),
            buffer((512, width), BF),
            buffer((2, 4, 64, width), BF),
            buffer((512, hidden), BF),
            buffer((512, hidden), BF),
            buffer((512, hidden), BF),
            buffer((4, 256, hidden), BF),
            buffer((3, 2, 128, hidden), BF),
            buffer((2, 2, 128, 640), BF),
            buffer((4, 256, 512), BF),
            buffer((4, 256, 640), BF),
            buffer((2, 64, hidden), F32),
            buffer((2, 128, 256), F32),
            buffer((2, 4, 64, width), BF),
            buffer((2, 3, 64, width), BF),
            buffer((2, 2, 64, width), BF),
            buffer((2, 3, 64, width), BF),
            buffer((2, 2, 64, width), BF),
            buffer((2, 4, 64, width), BF),
            buffer((64, width), F32),
            buffer((64, width), BF),
            buffer((2, 64, width), F32),
            buffer((2, 64, width), F32),
            buffer((512, 512), BF),
            buffer((2, 1024, 256), BF),
            buffer((16, 1, 256), F32),
            buffer((4, 512, 128), BF),
            buffer((512, 512), BF),
            buffer((512, 256), F32),
            buffer((256, 512), BF),
            buffer((2, 1024, 128), BF),
            buffer((2, HD, 1024), BF),
            buffer((1024, 128), BF),
            buffer((HD, 1024), BF),
            buffer((1024, 128), F32),
            buffer((1024, 128), F32),
            buffer((2, 4, 256, 128), BF),
            buffer((2, 3, 256, 128), BF),
            buffer((512, 640), BF),
            buffer((2, width), F32),
            buffer((4, 8, 8, 128), F32),
            buffer((8, 8, 128), F32),
            buffer((7, 8, 128), F32),
            dma((5, 9)),
            dma((5, 9)),
            dma((5,)),
            dma((10,)),
            dma((10,)),
            dma((3,)),
            dma((3,)),
            dma((4,)),
            dma((8, 3)),
            dma((8, 5)),
            dma((8, 5)),
            dma((8, 4)),
            dma((5, 10)),
            dma((5, 10)),
            pltpu.SemaphoreType.REGULAR((4,)),
            dma((2, 3)),
            dma((2, 3)),
            dma((10,)),
            dma((10,)),
            dma((2,)),
            dma((2, 2)),
            dma((2,)),
        ],
        compiler_params=pltpu.CompilerParams(
            collective_id=0, has_side_effects=True, vmem_limit_bytes=67043328
        ),
    )(
        tokens, jnp.stack([attn_gain, mlp_gain]), w_query, w_key.T, w_value.T, w_out, w_gate, w_up,
        w_down, cotangent, positions[None, :], segments[None, :], frequency,
    )


def hand_over_kernel(*refs):
    count = (len(refs) - 2) // 3
    sources, targets, buffers = refs[:count], refs[count : 2 * count], refs[2 * count : 3 * count]
    in_sem, out_sem = refs[3 * count :]
    fetch = [
        pltpu.make_async_copy(source, buffers[n], in_sem.at[n]) for n, source in enumerate(sources)
    ]
    store = [
        pltpu.make_async_copy(buffers[n], target, out_sem.at[n]) for n, target in enumerate(targets)
    ]
    for piece in fetch:
        piece.start()
    for n in range(count):
        fetch[n].wait()
        store[n].start()
    for piece in store:
        piece.wait()


def hand_over(values):
    anywhere = pl.BlockSpec(memory_space=pl.ANY)
    dma = pltpu.SemaphoreType.DMA
    return pl.pallas_call(
        hand_over_kernel,
        name="hand_over",
        out_shape=tuple(jax.ShapeDtypeStruct(value.shape, value.dtype) for value in values),
        in_specs=[anywhere] * len(values),
        out_specs=(anywhere,) * len(values),
        scratch_shapes=[pltpu.VMEM(value.shape, value.dtype) for value in values]
        + [dma((len(values),)), dma((len(values),))],
        compiler_params=pltpu.CompilerParams(vmem_limit_bytes=67043328),
    )(*values)


def fast_shards(tokens, *others):
    made = run_layer(tokens, *others)
    (
        query_g, out_g, gate_g, up_g, down_g, key_g, value_g, gain_one_g, gain_two_g, result, input_grad,
    ) = hand_over(made[4:5] + made[7:11] + made[5:7] + made[2:4] + made[0:2])
    return (
        result.reshape(tokens.shape),
        input_grad.reshape(tokens.shape),
        gain_one_g.reshape(-1),
        query_g,
        key_g.T,
        value_g.T,
        out_g,
        gain_two_g.reshape(-1),
        gate_g,
        up_g,
        down_g,
    )


def solution(mesh):
    in_specs = (
        P(("fsdp", "ctx"), None),
        P(("fsdp", "ctx")),
        P(("fsdp", "ctx"), "tp"),
        P(("fsdp", "ctx"), "tp"),
        P(("fsdp", "ctx"), "tp"),
        P("tp", ("fsdp", "ctx")),
        P(("fsdp", "ctx")),
        P(("fsdp", "ctx"), "tp"),
        P(("fsdp", "ctx"), "tp"),
        P("tp", ("fsdp", "ctx")),
        P(("fsdp", "ctx"), None),
        P(("fsdp", "ctx")),
        P(("fsdp", "ctx")),
    )
    out_specs = (
        P(("fsdp", "ctx"), None),
        P(("fsdp", "ctx"), None),
        P(("fsdp", "ctx")),
        P(("fsdp", "ctx"), "tp"),
        P(("fsdp", "ctx"), "tp"),
        P(("fsdp", "ctx"), "tp"),
        P("tp", ("fsdp", "ctx")),
        P(("fsdp", "ctx")),
        P(("fsdp", "ctx"), "tp"),
        P(("fsdp", "ctx"), "tp"),
        P("tp", ("fsdp", "ctx")),
    )
    small = (mesh.shape["fsdp"], mesh.shape["ctx"], mesh.shape["tp"]) == (2, 4, 4)
    return jax.shard_map(fast_shards if small else shards, mesh=mesh, in_specs=in_specs, out_specs=out_specs, check_vma=False)
```

profile of v0, /device:TPU:0, one launch (start us, length us, event | category | flops | bytes accessed | tf_op | source)
XLA Modules:
  0.0 304.7 jit_solution(2164657588485542786)
XLA Ops:
  0.6 0.7 stack.9
  1.3 0.7 stack.10
  2.0 0.6 pad_maximum_fusion.gains_in
  2.5 294.6 %decoder_layer.1 = (bf16[2,4,64,2048]{3,2,1,0:T(8,128)(2,1)}, bf16[2,4,64,2048]{3,2,1,0:T(8,128)(2,1)}, f32[2,128]{1,0:T(2,128)}, f32[2,128]{1,0:T(2,128)}, f32[...) custom-call(bf16[512,2048]{1,0:T(8,128)(2,1)} %tok_h.1, ...), custom_call_target="tpu_custom_call" | custom-call | tf_op jit(solution)/shard_map/decoder_layer/pallas_call | solution.py:1683
  297.1 7.4 %hand_over.1 = (f32[256,512]{1,0:T(8,128)}, f32[512,256]{1,0:T(8,128)}, f32[256,1408]{1,0:T(8,128)}, f32[256,1408]{1,0:T(8,128)}, f32[1408,256]{1,0:T(8,128)}, /...) custom-call(f32[256,512]{1,0:T(8,128)} %get-tuple-element.33.refs_0_, ...), custom_call_target="tpu_custom_call" | custom-call | tf_op jit(solution)/shard_map/hand_over/pallas_call | solution.py:1816
where the time goes:
time: 305 us
  Pallas kernels  302 us (99%)
    pallas_call x1, Pallas kernels, run_layer(): pl.pallas_call(layer_kernel, name='decoder_layer', out_shape=(shape((2, 4...  295 us
    pallas_call x1, Pallas kernels, hand_over(): pl.pallas_call(hand_over_kernel, name='hand_over', out_shape=tuple((jax.S...  7.38 us

commit v1 on v0

--- a/solution.py
+++ b/solution.py
@@ -400,13 +400,6 @@
         )
 
 
-def greet(devices):
-    barrier = pltpu.get_barrier_semaphore()
-    for device in devices:
-        pl.semaphore_signal(barrier, inc=1, device_id=device, device_id_type=MESH)
-    pl.semaphore_wait(barrier, len(devices))
-
-
 def group_devices(me):
     return [
         me.at(c=me.cx),
@@ -821,7 +814,8 @@
 
 def layer_kernel(
     tok_h,
-    gains_in,
+    gain_one_in,
+    gain_two_in,
     w_query_in,
     w_key_in,
     w_value_in,
@@ -936,16 +930,20 @@
     load_one = pltpu.make_async_copy(n_one_h, mlow, load_sem.at[3])
     load_tok.start()
     load_cot.start()
+    barrier = pltpu.get_barrier_semaphore()
+    for device in group + column_devices(me):
+        pl.semaphore_signal(barrier, inc=1, device_id=device, device_id_type=MESH)
 
     w_qkv[me.own, :, 0:512] = w_query_in[...]
     turned = jnp.concatenate([w_key_in[...], w_value_in[...]], axis=0).astype(F32)
     w_qkv[me.own, :, 512:640] = jnp.transpose(turned).astype(BF)
-    own_gains[0:2, :] = gains_in[...].astype(F32)
+    own_gains[0:1, :] = gain_one_in[...].reshape(1, 256).astype(F32)
+    own_gains[1:2, :] = gain_two_in[...].reshape(1, 256).astype(F32)
     own_gains[2:8, :] = jnp.zeros((6, 256), F32)
     own_marks[0:1, :] = pos_in[...]
     own_marks[1:2, :] = seg_in[...]
     own_marks[2:8, :] = jnp.zeros((6, 512), jnp.int32)
-    greet(group + column_devices(me))
+    pl.semaphore_wait(barrier, 10)
 
     qkv = Gather(me, 0, None, w_qkv, g_send, g_recv, g_local)
     out = Gather(me, 1, out_h, w_out, g_send, g_recv, g_local)
@@ -1482,8 +1480,8 @@
             piece.wait_send()
 
     order = (
+        (qkv.begin,),
         (small_begin,),
-        (qkv.begin,),
         (make_rope,),
         (qkv.forward_a,),
         (qkv.forward_b,),
@@ -1702,7 +1700,7 @@
             shape((2, 256, 640), BF),
             shape((2, 4, 64, width), BF),
         ),
-        in_specs=[anywhere, vmem, vmem, vmem, vmem]
+        in_specs=[anywhere, vmem, vmem, vmem, vmem, vmem]
         + [anywhere] * 5
         + [vmem] * 3,
         out_specs=(anywhere,) * 2 + (vmem,) * 2 + (anywhere,) * 13,
@@ -1786,7 +1784,7 @@
             collective_id=0, has_side_effects=True, vmem_limit_bytes=67043328
         ),
     )(
-        tokens, jnp.stack([attn_gain, mlp_gain]), w_query, w_key.T, w_value.T, w_out, w_gate, w_up,
+        tokens, attn_gain, mlp_gain, w_query, w_key.T, w_value.T, w_out, w_gate, w_up,
         w_down, cotangent, positions[None, :], segments[None, :], frequency,
     )
 

time: 305 us -> 302 us (level)
  no operation moved by 1% of the time
where the time goes in v1:
time: 302 us
  Pallas kernels  301 us (100%)
    pallas_call x1, Pallas kernels, run_layer(): pl.pallas_call(layer_kernel, name='decoder_layer', out_shape=(shape((2, 4...  294 us
    pallas_call x1, Pallas kernels, hand_over(): pl.pallas_call(hand_over_kernel, name='hand_over', out_shape=tuple((jax.S...  7.38 us

profile of v1, /device:TPU:0, one launch (start us, length us, event | category | flops | bytes accessed | tf_op | source)
XLA Modules:
  0.0 302.1 jit_solution(832779411626303565)
XLA Ops:
  0.6 293.9 %decoder_layer.1 = (bf16[2,4,64,2048]{3,2,1,0:T(8,128)(2,1)}, bf16[2,4,64,2048]{3,2,1,0:T(8,128)(2,1)}, f32[2,128]{1,0:T(2,128)}, f32[2,128]{1,0:T(2,128)}, f32[...) custom-call(bf16[512,2048]{1,0:T(8,128)(2,1)} %tok_h.1, ...), custom_call_target="tpu_custom_call" | custom-call | tf_op jit(solution)/shard_map/decoder_layer/pallas_call | solution.py:1681
  294.5 7.4 %hand_over.1 = (f32[256,512]{1,0:T(8,128)}, f32[512,256]{1,0:T(8,128)}, f32[256,1408]{1,0:T(8,128)}, f32[256,1408]{1,0:T(8,128)}, f32[1408,256]{1,0:T(8,128)}, /...) custom-call(f32[256,512]{1,0:T(8,128)} %get-tuple-element.33.refs_0_, ...), custom_call_target="tpu_custom_call" | custom-call | tf_op jit(solution)/shard_map/hand_over/pallas_call | solution.py:1814

commit v2 on v1

--- a/solution.py
+++ b/solution.py
@@ -586,14 +586,18 @@
                 + self.outer_in[2].astype(F32)
                 + self.inner_in[1].astype(F32)
             )
-            for piece in self.mid_copies():
-                piece.wait_send()
 
         @pl.when(self.is_end)
         def _():
             self.wait_in(3, self.inner_in.at[0])
             total[...] = self.part[me.z].astype(F32) + self.inner_in[0].astype(F32)
             for piece in self.end_copies():
+                piece.wait_send()
+
+    def drain(self):
+        @pl.when(self.is_mid)
+        def _():
+            for piece in self.mid_copies():
                 piece.wait_send()
 
 
@@ -1143,6 +1147,8 @@
         ).astype(BF)
 
     def feed_back(g):
+        sum_att[g].drain()
+
         def body(shard, carry):
             term = dotg(gate_g[rows_of[g], :], w_gate[shard], 1, 1) + dotg(
                 up_g[rows_of[g], :], w_up[shard], 1, 1
@@ -1406,6 +1412,8 @@
         d_qkv[rows_of[g], 512:640] = rows.astype(BF)
 
     def project_back_rows(g):
+        sum_two[g].drain()
+
         def body(shard, carry):
             term = dotg(d_qkv[rows_of[g], :], w_qkv[shard], 1, 1)
             part[g, :, :, pl.ds(pl.multiple_of(shard * 256, 256), 256)] = term.astype(BF).reshape(
@@ -1469,6 +1477,8 @@
             piece.settle()
 
     def settle():
+        for job in sum_one + sum_out:
+            job.drain()
         for spread in spread_in + spread_out:
             spread.finish()
         for job in (rs_down, rs_gate, rs_up, rs_out, rs_qkv):

time: 302 us -> 302 us (level)
  no operation moved by 1% of the time
where the time goes in v2:
time: 302 us; the launch traced here: 301 us
  Pallas kernels  301 us (100%)
    pallas_call x1, Pallas kernels, run_layer(): pl.pallas_call(layer_kernel, name='decoder_layer', out_shape=(shape((2, 4...  293 us
    pallas_call x1, Pallas kernels, hand_over(): pl.pallas_call(hand_over_kernel, name='hand_over', out_shape=tuple((jax.S...  7.38 us

profile of v2, /device:TPU:0, one launch (start us, length us, event | category | flops | bytes accessed | tf_op | source)
XLA Modules:
  0.0 301.4 jit_solution(703926919312259186)
XLA Ops:
  0.6 293.2 %decoder_layer.1 = (bf16[2,4,64,2048]{3,2,1,0:T(8,128)(2,1)}, bf16[2,4,64,2048]{3,2,1,0:T(8,128)(2,1)}, f32[2,128]{1,0:T(2,128)}, f32[2,128]{1,0:T(2,128)}, f32[...) custom-call(bf16[512,2048]{1,0:T(8,128)(2,1)} %tok_h.1, ...), custom_call_target="tpu_custom_call" | custom-call | tf_op jit(solution)/shard_map/decoder_layer/pallas_call | solution.py:1691
  293.9 7.4 %hand_over.1 = (f32[256,512]{1,0:T(8,128)}, f32[512,256]{1,0:T(8,128)}, f32[256,1408]{1,0:T(8,128)}, f32[256,1408]{1,0:T(8,128)}, f32[1408,256]{1,0:T(8,128)}, /...) custom-call(f32[256,512]{1,0:T(8,128)} %get-tuple-element.33.refs_0_, ...), custom_call_target="tpu_custom_call" | custom-call | tf_op jit(solution)/shard_map/hand_over/pallas_call | solution.py:1824

commit v3 on v2

--- a/solution.py
+++ b/solution.py
@@ -1803,17 +1803,20 @@
     count = (len(refs) - 2) // 3
     sources, targets, buffers = refs[:count], refs[count : 2 * count], refs[2 * count : 3 * count]
     in_sem, out_sem = refs[3 * count :]
-    fetch = [
-        pltpu.make_async_copy(source, buffers[n], in_sem.at[n]) for n, source in enumerate(sources)
-    ]
-    store = [
-        pltpu.make_async_copy(buffers[n], target, out_sem.at[n]) for n, target in enumerate(targets)
-    ]
+    fetch, store = [], []
+    for n in range(count):
+        rows = sources[n].shape[0]
+        cut = rows // 2 if rows >= 256 or len(sources[n].shape) == 4 else rows
+        for part, first in enumerate(range(0, rows, cut)):
+            piece = pl.ds(first, cut)
+            held = buffers[n].at[piece]
+            fetch.append(pltpu.make_async_copy(sources[n].at[piece], held, in_sem.at[n, part]))
+            store.append(pltpu.make_async_copy(held, targets[n].at[piece], out_sem.at[n, part]))
     for piece in fetch:
         piece.start()
-    for n in range(count):
-        fetch[n].wait()
-        store[n].start()
+    for arrival, leave in zip(fetch, store):
+        arrival.wait()
+        leave.start()
     for piece in store:
         piece.wait()
 
@@ -1828,7 +1831,7 @@
         in_specs=[anywhere] * len(values),
         out_specs=(anywhere,) * len(values),
         scratch_shapes=[pltpu.VMEM(value.shape, value.dtype) for value in values]
-        + [dma((len(values),)), dma((len(values),))],
+        + [dma((len(values), 2)), dma((len(values), 2))],
         compiler_params=pltpu.CompilerParams(vmem_limit_bytes=67043328),
     )(*values)
 

time: 302 us -> 302 us (level)
  no operation moved by 1% of the time
where the time goes in v3:
time: 302 us
  Pallas kernels  301 us (100%)
    pallas_call x1, Pallas kernels, run_layer(): pl.pallas_call(layer_kernel, name='decoder_layer', out_shape=(shape((2, 4...  293 us
    pallas_call x1, Pallas kernels, hand_over(): pl.pallas_call(hand_over_kernel, name='hand_over', out_shape=tuple((jax.S...  7.82 us

profile of v3, /device:TPU:0, one launch (start us, length us, event | category | flops | bytes accessed | tf_op | source)
XLA Modules:
  0.0 301.9 jit_solution(2647529925273511939)
XLA Ops:
  0.6 293.2 %decoder_layer.1 = (bf16[2,4,64,2048]{3,2,1,0:T(8,128)(2,1)}, bf16[2,4,64,2048]{3,2,1,0:T(8,128)(2,1)}, f32[2,128]{1,0:T(2,128)}, f32[2,128]{1,0:T(2,128)}, f32[...) custom-call(bf16[512,2048]{1,0:T(8,128)(2,1)} %tok_h.1, ...), custom_call_target="tpu_custom_call" | custom-call | tf_op jit(solution)/shard_map/decoder_layer/pallas_call | solution.py:1691
  293.9 7.8 %hand_over.1 = (f32[256,512]{1,0:T(8,128)}, f32[512,256]{1,0:T(8,128)}, f32[256,1408]{1,0:T(8,128)}, f32[256,1408]{1,0:T(8,128)}, f32[1408,256]{1,0:T(8,128)}, /...) custom-call(f32[256,512]{1,0:T(8,128)} %get-tuple-element.33.refs_0_, ...), custom_call_target="tpu_custom_call" | custom-call | tf_op jit(solution)/shard_map/hand_over/pallas_call | solution.py:1827
